TPU v7x, 32 devices: a whole 2x2x4 slice. The times are simulated.
32 devices in a mesh: gx: 8 (over z, y), gy: 4 (over x, core).
Axes of the slice: x: 2, y: 2, z: 4, core: 2. Of those that a mesh axis runs over, the one named last changes fastest.
Arguments:
- cell_state: float32 [39, 65536], P(None, ('gx', 'gy')), may hold values from 0.1 to 2
- coupling: float32 [39, 39], replicated, may hold values from -1 to 1
- basal_rate: float32 [39], replicated, may hold values from 0.1 to 1
- half_sat: float32 [39], replicated, may hold values from 0.2 to 2
- decay_rate: float32 [39], replicated, may hold values from 0.1 to 1
- uptake_weight: float32 [39], replicated, may hold values from -1 to 1
- agent_counts: int32 [32], P(('gx', 'gy')), may hold values from 512 to 2048, as said below
- divider_ids: int32 [4096], P(('gx', 'gy')), may hold values from 0 to 2047, as said below
- destinations: int32 [4096, 1], P(('gx', 'gy')), may hold values from 0 to 7; in each aligned block of 128 rows (0 to 127, 128 to 255, ...) at most 32 rows name the same one
- voxel_index: int32 [65536], P(('gx', 'gy')), may hold values from 0 to 196607, as said below
- oxygen: float32 [64, 64, 512], P(None, 'gx', 'gy'), may hold values from 0.5 to 1.5
Outputs:
- new_state: float32 [39, 65536], P(None, ('gx', 'gy'))
- daughter_state: float32 [39, 8192], P(None, ('gx', 'gy'))
- new_oxygen: float32 [64, 64, 512], P(None, 'gx', 'gy')
Inputs may be any that keep to these rules, and one draw needn't show every extreme that they name: Live agents of a device are its first agent_counts slots; at least 512, and some device holds 2048. `divider_ids`: each entry is below the live count of its device; entries may repeat. `destinations`: within the list of one device no x-slab is named by more than 32 rows. `voxel_index`: the named voxel lies in the agent's own x-slab or an adjacent one (s = 0, 1 or 2) and inside the grid, with y inside its device's range.
All inputs are finite; a program needn't handle non-finite values.
Results may differ from a plain program's by a relative error of at most 0.0011.
Values may be sent and summed in bfloat16 or wider, within the bound.
No kernel may reach another device: no remote copies, remote signals or barrier semaphores. Data moves between devices by JAX's collectives and lax.ppermute only.
A program may use at most 64 MiB of HBM per device.

v0:
```python
import math
import jax
import jax.numpy as jnp
from jax import lax
from jax.sharding import PartitionSpec as P

time_step = 0.25
diffusion_number = 0.16


def shifted(block, axis, distance):
    devices = range(lax.axis_size(axis))
    route = [(i - distance, i) for i in devices if i - distance in devices]
    return lax.ppermute(block, axis, route)


def with_halo(cells, sides, width):
    for axis, dim in sides:
        count = lax.axis_size(axis)
        ends = count - 1
        head = lax.slice_in_dim(cells, 0, width, axis=dim)
        tail = lax.slice_in_dim(cells, cells.shape[dim] - width, cells.shape[dim], axis=dim)
        cells = jnp.concatenate(
            [
                lax.ppermute(tail, axis, [(i, (i + 1) % count) for i in range(ends)]),
                cells,
                lax.ppermute(head, axis, [((i + 1) % count, i) for i in range(ends)]),
            ],
            axis=dim,
        )
    return cells


def network_rates(current, coupling, basal_rate, half_sat, decay_rate):
    square = current * current
    occupancy = square / (half_sat[:, None] * half_sat[:, None] + square)
    drive_sum = jnp.dot(
        coupling, occupancy, precision=lax.Precision.HIGHEST, preferred_element_type=jnp.float32
    )
    return basal_rate[:, None] + drive_sum - decay_rate[:, None] * current


def advance(current, coupling, basal_rate, half_sat, decay_rate):
    for substep in range(2):
        middle = current + 0.5 * time_step * network_rates(
            current, coupling, basal_rate, half_sat, decay_rate
        )
        current = current + time_step * network_rates(
            middle, coupling, basal_rate, half_sat, decay_rate
        )
    return current


def deposit_rows(weights, row_index, columns, row_count, column_count):
    block_size = math.gcd(weights.shape[0], 512)
    block_count = weights.shape[0] // block_size
    row_ids = jnp.arange(row_count, dtype=jnp.int32)
    column_ids = jnp.arange(column_count, dtype=jnp.int32)

    def one_block(running, block_turn):
        start = block_turn * block_size
        piece_weight = lax.dynamic_slice_in_dim(weights, start, block_size)
        piece_row = lax.dynamic_slice_in_dim(row_index, start, block_size)
        piece_column = lax.dynamic_slice_in_dim(columns, start, block_size)
        left_table = (piece_row[:, None] == row_ids[None, :]).astype(jnp.bfloat16)
        right_table = (piece_column[:, None] == column_ids[None, :]).astype(
            jnp.bfloat16
        ) * piece_weight[:, None]
        product = lax.dot_general(
            left_table, right_table, (((0,), (0,)), ((), ())), preferred_element_type=jnp.float32
        )
        return (running + product, None)

    running, unused = lax.scan(
        one_block, jnp.zeros((row_count, column_count), jnp.float32), jnp.arange(block_count)
    )
    return running


def sweep_once(padded):
    z_padded = jnp.pad(padded, ((1, 1), (0, 0), (0, 0)))
    center = padded[:, 1:-1, 1:-1]
    beside = z_padded[2:, 1:-1, 1:-1] + z_padded[:-2, 1:-1, 1:-1]
    beside = beside + padded[:, 2:, 1:-1] + padded[:, :-2, 1:-1]
    beside = beside + padded[:, 1:-1, 2:] + padded[:, 1:-1, :-2]
    return center + diffusion_number * (beside - 6.0 * center)


def shards(
    cell_state,
    coupling,
    basal_rate,
    half_sat,
    decay_rate,
    uptake_weight,
    agent_counts,
    divider_ids,
    destinations,
    voxel_index,
    oxygen,
):
    grid_count = lax.axis_size("gx")
    picks_count = divider_ids.shape[0]
    capacity = max(2, 2 * picks_count // grid_count)
    target_slab = destinations[:, 0]
    onehot = (target_slab[:, None] == jnp.arange(grid_count, dtype=jnp.int32)[None, :]).astype(
        jnp.int32
    )
    earlier = jnp.cumsum(onehot, axis=0) - onehot
    slot_rank = jnp.sum(earlier * onehot, axis=1)
    position = target_slab * capacity + slot_rank
    placing = (
        position[:, None] == jnp.arange(grid_count * capacity, dtype=jnp.int32)[None, :]
    ).astype(jnp.float32)
    mothers = jnp.take(cell_state, divider_ids, axis=1)
    outgoing = jnp.dot(
        mothers, placing, precision=lax.Precision.HIGHEST, preferred_element_type=jnp.float32
    )
    occupied = jnp.sum(placing, axis=0)[None, :]
    received, arrived = (
        lax.all_to_all(outgoing, "gx", split_axis=1, concat_axis=1, tiled=True),
        lax.all_to_all(occupied, "gx", split_axis=1, concat_axis=1, tiled=True),
    )
    new_state = advance(cell_state, coupling, basal_rate, half_sat, decay_rate)
    daughter_state = advance(received, coupling, basal_rate, half_sat, decay_rate) * arrived
    agents = cell_state.shape[1]
    drive_sum = jnp.dot(
        uptake_weight,
        new_state,
        precision=lax.Precision.HIGHEST,
        preferred_element_type=jnp.float32,
    )
    alive_mask = jnp.arange(agents, dtype=jnp.int32) < agent_counts[0]
    uptake = jnp.where(alive_mask, jax.nn.softplus(drive_sum), 0.0).astype(jnp.bfloat16)
    depth_cells, width_x, width_y = oxygen.shape
    slab_rows = depth_cells * width_x
    row_index = voxel_index // width_y
    columns = voxel_index % width_y
    partial_value = deposit_rows(uptake, row_index, columns, 3 * slab_rows, width_y).reshape(
        3, depth_cells, width_x, width_y
    )
    from_lower = shifted(partial_value[2].astype(jnp.bfloat16), "gx", 1).astype(jnp.float32)
    from_upper = shifted(partial_value[0].astype(jnp.bfloat16), "gx", -1).astype(jnp.float32)
    deposit = partial_value[1] + from_lower + from_upper
    oxygen_field = oxygen - deposit
    for sweep_turn in range(4):
        padded = with_halo(oxygen_field, (("gx", 1), ("gy", 2)), 1)
        oxygen_field = sweep_once(padded)
    return (new_state, daughter_state, oxygen_field)


def solution(mesh):
    return jax.shard_map(
        shards,
        mesh=mesh,
        in_specs=(
            P(None, ("gx", "gy")),
            P(),
            P(),
            P(),
            P(),
            P(),
            P(("gx", "gy")),
            P(("gx", "gy")),
            P(("gx", "gy"), None),
            P(("gx", "gy")),
            P(None, "gx", "gy"),
        ),
        out_specs=(P(None, ("gx", "gy")), P(None, ("gx", "gy")), P(None, "gx", "gy")),
        check_vma=False,
    )
```

profile of v0, /device:TPU:1, one launch (start us, length us, event | category | flops | bytes accessed | tf_op | source)
XLA Modules:
  0.0 136.2 jit_solution(7530949191528294205)
XLA Ops:
  6.1 12.0 %while.11 = (s32[]{:T(128)}, f32[1536,128]{1,0:T(8,128)S(1)}, s32[4]{0:T(128)S(1)}, s32[2048]{0:T(1024)S(1)}, s32[2048]{0:T(1024)S(1)}, /*index=5*/bf16[2048]{0:...) while((s32[]{:T(128)}, f32[1536,128]{1,0:T(8,128)S(1)}, s32[4]{0:T(128)S(1)}, ...), condition=%wide.region_4.5_spmd.clone, body=%wide.region_3.4_spmd.clone.sunk | while | flops 202637312 | bytes 1588405 | solution.py:74
  18.2 4.0 %collective-permute-start = (bf16[64,8,128]{2,1,0:T(8,128)(2,1)S(1)}, bf16[64,8,128]{2,1,0:T(8,128)(2,1)S(1)}, u32[]{:S(2)}, u32[]{:S(2)}) collective-permute-start(bf16[64,8,128]{2,1,0:T(8,128)(2,1)S(1)} %get-tuple-element.91), channel_id=1, source_target_pairs={{0,4},{4,8},{8,12},{12,16},{16,20},{20,24},{24,28},{1,5},{5,9},{9,... | collective-permute-start | bytes 393224 | tf_op jit(solution)/shard_map/ppermute | solution.py:14
  24.7 6.4 %all-to-all-start.1 = ((f32[1,8,32]{2,0,1:T(1,128)}), f32[1,8,32]{2,0,1:T(1,128)S(1)}, u32[]{:S(2)}, u32[]{:S(2)}) async-start(f32[1,8,32]{2,0,1:T(1,128)} %all_to_all.17), calls=%async_computation.1 | async-start | bytes 8192 | tf_op jit(solution)/shard_map/all_to_all | solution.py:122
  31.3 3.4 %collective-permute-start.2 = (f32[64,1,128]{2,1,0:T(1,128)S(1)}, f32[64,1,128]{2,1,0:T(1,128)S(1)}, u32[]{:S(2)}, u32[]{:S(2)}) collective-permute-start(f32[64,1,128]{2,1,0:T(1,128)S(1)} %get-tuple-element.99), channel_id=1, source_target_pairs={{0,4},{4,8},{8,12},{12,16},{16,20},{20,24},{24,28},{1,5},{5,9},{9,... | collective-permute-start | bytes 98312 | tf_op jit(solution)/shard_map/ppermute | solution.py:25
  36.0 3.3 %collective-permute-done.3 = f32[64,1,128]{2,1,0:T(1,128)S(1)} collective-permute-done((f32[64,1,128]{2,1,0:T(1,128)S(1)}, f32[64,1,128]{2,1,0:T(1,128)S(1)}, u32[]{:S(2)}, u32[]{:S(2)}) %collective-permute-start.3) | collective-permute-done | bytes 32800 | tf_op jit(solution)/shard_map/ppermute | solution.py:27
  40.5 6.2 %collective-permute-start.4 = (f32[64,10,1]{2,1,0:T(8,128)}, f32[64,10,1]{2,1,0:T(8,128)S(1)}, u32[]{:S(2)}, u32[]{:S(2)}) collective-permute-start(f32[64,10,1]{2,1,0:T(8,128)} %get-tuple-element.90), channel_id=1, source_target_pairs={{0,1},{1,2},{2,3},{4,5},{5,6},{6,7},{8,9},{9,10},{10,11},{12,13},{... | collective-permute-start | bytes 7688 | tf_op jit(solution)/shard_map/ppermute | solution.py:25
  46.7 1.9 %collective-permute-start.5 = (f32[64,10,1]{2,1,0:T(8,128)S(1)}, f32[64,10,1]{2,1,0:T(8,128)S(1)}, u32[]{:S(2)}, u32[]{:S(2)}) collective-permute-start(f32[64,10,1]{2,1,0:T(8,128)S(1)} %get-tuple-element.89), channel_id=1, source_target_pairs={{1,0},{2,1},{3,2},{5,4},{6,5},{7,6},{9,8},{10,9},{11,10},{13,12},{... | collective-permute-start | bytes 7688 | tf_op jit(solution)/shard_map/ppermute | solution.py:27
  49.7 3.5 %collective-permute-done.4 = f32[64,10,1]{2,1,0:T(8,128)S(1)} collective-permute-done((f32[64,10,1]{2,1,0:T(8,128)}, f32[64,10,1]{2,1,0:T(8,128)S(1)}, u32[]{:S(2)}, u32[]{:S(2)}) %collective-permute-start.4) | collective-permute-done | bytes 2592 | tf_op jit(solution)/shard_map/ppermute | solution.py:25
  53.1 4.1 %collective-permute-done.5 = f32[64,10,1]{2,1,0:T(8,128)S(1)} collective-permute-done((f32[64,10,1]{2,1,0:T(8,128)S(1)}, f32[64,10,1]{2,1,0:T(8,128)S(1)}, u32[]{:S(2)}, u32[]{:S(2)}) %collective-permute-start.5) | collective-permute-done | bytes 2592 | tf_op jit(solution)/shard_map/ppermute | solution.py:27
  59.3 4.0 %collective-permute-start.6 = (f32[64,1,128]{2,1,0:T(1,128)S(1)}, f32[64,1,128]{2,1,0:T(1,128)S(1)}, u32[]{:S(2)}, u32[]{:S(2)}) collective-permute-start(f32[64,1,128]{2,1,0:T(1,128)S(1)} %get-tuple-element.97), channel_id=1, source_target_pairs={{0,4},{4,8},{8,12},{12,16},{16,20},{20,24},{24,28},{1,5},{5,9},{9,... | collective-permute-start | bytes 98312 | tf_op jit(solution)/shard_map/ppermute | solution.py:25
  65.8 2.2 %collective-permute-done.7 = f32[64,1,128]{2,1,0:T(1,128)S(1)} collective-permute-done((f32[64,1,128]{2,1,0:T(1,128)S(1)}, f32[64,1,128]{2,1,0:T(1,128)S(1)}, u32[]{:S(2)}, u32[]{:S(2)}) %collective-permute-start.7) | collective-permute-done | bytes 32800 | tf_op jit(solution)/shard_map/ppermute | solution.py:27
  68.1 4.3 %all-to-all-start = ((f32[8,1,1248]{2,1,0:T(1,128)}), f32[8,1,1248]{2,1,0:T(1,128)S(1)}, u32[]{:S(2)}, u32[]{:S(2)}) async-start(f32[8,1,1248]{2,1,0:T(1,128)} %reshape.58), calls=%async_computation | async-start | bytes 81920 | tf_op jit(solution)/shard_map/all_to_all | solution.py:121
  72.6 3.5 %collective-permute-start.8 = (f32[64,10,1]{2,1,0:T(8,128)S(1)}, f32[64,10,1]{2,1,0:T(8,128)S(1)}, u32[]{:S(2)}, u32[]{:S(2)}) collective-permute-start(f32[64,10,1]{2,1,0:T(8,128)S(1)} %get-tuple-element.88), channel_id=1, source_target_pairs={{0,1},{1,2},{2,3},{4,5},{5,6},{6,7},{8,9},{9,10},{10,11},{12,13},{... | collective-permute-start | bytes 7688 | tf_op jit(solution)/shard_map/ppermute | solution.py:25
  82.2 4.4 %collective-permute-done.9 = f32[64,10,1]{2,1,0:T(8,128)S(1)} collective-permute-done((f32[64,10,1]{2,1,0:T(8,128)S(1)}, f32[64,10,1]{2,1,0:T(8,128)S(1)}, u32[]{:S(2)}, u32[]{:S(2)}) %collective-permute-start.9) | collective-permute-done | bytes 2592 | tf_op jit(solution)/shard_map/ppermute | solution.py:27
  88.0 3.7 %collective-permute-start.10 = (f32[64,1,128]{2,1,0:T(1,128)S(1)}, f32[64,1,128]{2,1,0:T(1,128)S(1)}, u32[]{:S(2)}, u32[]{:S(2)}) collective-permute-start(f32[64,1,128]{2,1,0:T(1,128)S(1)} %get-tuple-element.95), channel_id=1, source_target_pairs={{0,4},{4,8},{8,12},{12,16},{16,20},{20,24},{24,28},{1,5},{5,9},{9,... | collective-permute-start | bytes 98312 | tf_op jit(solution)/shard_map/ppermute | solution.py:25
  93.3 3.1 %collective-permute-done.11 = f32[64,1,128]{2,1,0:T(1,128)S(1)} collective-permute-done((f32[64,1,128]{2,1,0:T(1,128)S(1)}, f32[64,1,128]{2,1,0:T(1,128)S(1)}, u32[]{:S(2)}, u32[]{:S(2)}) %collective-permute-start.11) | collective-permute-done | bytes 32800 | tf_op jit(solution)/shard_map/ppermute | solution.py:27
  96.7 3.1 %collective-permute-start.12 = (f32[64,10,1]{2,1,0:T(8,128)S(1)}, f32[64,10,1]{2,1,0:T(8,128)S(1)}, u32[]{:S(2)}, u32[]{:S(2)}) collective-permute-start(f32[64,10,1]{2,1,0:T(8,128)S(1)} %get-tuple-element.86), channel_id=1, source_target_pairs={{0,1},{1,2},{2,3},{4,5},{5,6},{6,7},{8,9},{9,10},{10,11},{12,13},{... | collective-permute-start | bytes 7688 | tf_op jit(solution)/shard_map/ppermute | solution.py:25
  101.9 3.9 %collective-permute-done.12 = f32[64,10,1]{2,1,0:T(8,128)S(1)} collective-permute-done((f32[64,10,1]{2,1,0:T(8,128)S(1)}, f32[64,10,1]{2,1,0:T(8,128)S(1)}, u32[]{:S(2)}, u32[]{:S(2)}) %collective-permute-start.12) | collective-permute-done | bytes 2592 | tf_op jit(solution)/shard_map/ppermute | solution.py:25
  105.9 4.4 %collective-permute-done.13 = f32[64,10,1]{2,1,0:T(8,128)S(1)} collective-permute-done((f32[64,10,1]{2,1,0:T(8,128)S(1)}, f32[64,10,1]{2,1,0:T(8,128)S(1)}, u32[]{:S(2)}, u32[]{:S(2)}) %collective-permute-start.13) | collective-permute-done | bytes 2592 | tf_op jit(solution)/shard_map/ppermute | solution.py:27
  111.6 4.1 %collective-permute-start.14 = (f32[64,1,128]{2,1,0:T(1,128)S(1)}, f32[64,1,128]{2,1,0:T(1,128)S(1)}, u32[]{:S(2)}, u32[]{:S(2)}) collective-permute-start(f32[64,1,128]{2,1,0:T(1,128)S(1)} %get-tuple-element.93), channel_id=1, source_target_pairs={{0,4},{4,8},{8,12},{12,16},{16,20},{20,24},{24,28},{1,5},{5,9},{9,... | collective-permute-start | bytes 98312 | tf_op jit(solution)/shard_map/ppermute | solution.py:25
  117.3 3.1 %collective-permute-done.15 = f32[64,1,128]{2,1,0:T(1,128)S(1)} collective-permute-done((f32[64,1,128]{2,1,0:T(1,128)S(1)}, f32[64,1,128]{2,1,0:T(1,128)S(1)}, u32[]{:S(2)}, u32[]{:S(2)}) %collective-permute-start.15) | collective-permute-done | bytes 32800 | tf_op jit(solution)/shard_map/ppermute | solution.py:27
  120.6 3.1 %collective-permute-start.16 = (f32[64,10,1]{2,1,0:T(8,128)S(1)}, f32[64,10,1]{2,1,0:T(8,128)S(1)}, u32[]{:S(2)}, u32[]{:S(2)}) collective-permute-start(f32[64,10,1]{2,1,0:T(8,128)S(1)} %get-tuple-element.84), channel_id=1, source_target_pairs={{0,1},{1,2},{2,3},{4,5},{5,6},{6,7},{8,9},{9,10},{10,11},{12,13},{... | collective-permute-start | bytes 7688 | tf_op jit(solution)/shard_map/ppermute | solution.py:25
  126.5 3.3 %collective-permute-done.16 = f32[64,10,1]{2,1,0:T(8,128)S(1)} collective-permute-done((f32[64,10,1]{2,1,0:T(8,128)S(1)}, f32[64,10,1]{2,1,0:T(8,128)S(1)}, u32[]{:S(2)}, u32[]{:S(2)}) %collective-permute-start.16) | collective-permute-done | bytes 2592 | tf_op jit(solution)/shard_map/ppermute | solution.py:25
  129.8 4.4 %collective-permute-done.17 = f32[64,10,1]{2,1,0:T(8,128)S(1)} collective-permute-done((f32[64,10,1]{2,1,0:T(8,128)S(1)}, f32[64,10,1]{2,1,0:T(8,128)S(1)}, u32[]{:S(2)}, u32[]{:S(2)}) %collective-permute-start.17) | collective-permute-done | bytes 2592 | tf_op jit(solution)/shard_map/ppermute | solution.py:27
  (118 shorter events, 44.3 us)
Async XLA Ops:
  18.1 13.0 %copy-start.9 = (s32[128]{0:T(128)S(1)}, s32[128]{0:T(128)}, u32[]{:S(2)}) copy-start(s32[128]{0:T(128)} %param.20) | copy-start | bytes 1540
  18.1 13.1 %copy-start.5 = (f32[64,8,128]{2,1,0:T(8,128)S(1)}, f32[64,8,128]{2,1,0:T(8,128)}, u32[]{:S(2)}) copy-start(f32[64,8,128]{2,1,0:T(8,128)} %param.23) | copy-start | bytes 786436
  18.2 13.0 %collective-permute-start = (bf16[64,8,128]{2,1,0:T(8,128)(2,1)S(1)}, bf16[64,8,128]{2,1,0:T(8,128)(2,1)S(1)}, u32[]{:S(2)}, u32[]{:S(2)}) collective-permute-start(bf16[64,8,128]{2,1,0:T(8,128)(2,1)S(1)} %get-tuple-element.91), channel_id=1, source_target_pairs={{0,4},{4,8},{8,12},{12,16},{16,20},{20,24},{24,28},{1,5},{5,9},{9,... | collective-permute-start | bytes 393224 | tf_op jit(solution)/shard_map/ppermute | solution.py:14
  22.2 9.0 %collective-permute-start.1 = (bf16[64,8,128]{2,1,0:T(8,128)(2,1)S(1)}, bf16[64,8,128]{2,1,0:T(8,128)(2,1)S(1)}, u32[]{:S(2)}, u32[]{:S(2)}) collective-permute-start(bf16[64,8,128]{2,1,0:T(8,128)(2,1)S(1)} %get-tuple-element.92), channel_id=1, source_target_pairs={{4,0},{8,4},{12,8},{16,12},{20,16},{24,20},{28,24},{5,1},{9,5},{13... | collective-permute-start | bytes 393224 | tf_op jit(solution)/shard_map/ppermute | solution.py:14
  24.7 43.4 %all-to-all-start.1 = ((f32[1,8,32]{2,0,1:T(1,128)}), f32[1,8,32]{2,0,1:T(1,128)S(1)}, u32[]{:S(2)}, u32[]{:S(2)}) async-start(f32[1,8,32]{2,0,1:T(1,128)} %all_to_all.17), calls=%async_computation.1 | async-start | bytes 8192 | tf_op jit(solution)/shard_map/all_to_all | solution.py:122
  31.3 4.7 %collective-permute-start.2 = (f32[64,1,128]{2,1,0:T(1,128)S(1)}, f32[64,1,128]{2,1,0:T(1,128)S(1)}, u32[]{:S(2)}, u32[]{:S(2)}) collective-permute-start(f32[64,1,128]{2,1,0:T(1,128)S(1)} %get-tuple-element.99), channel_id=1, source_target_pairs={{0,4},{4,8},{8,12},{12,16},{16,20},{20,24},{24,28},{1,5},{5,9},{9,... | collective-permute-start | bytes 98312 | tf_op jit(solution)/shard_map/ppermute | solution.py:25
  34.7 4.7 %collective-permute-start.3 = (f32[64,1,128]{2,1,0:T(1,128)S(1)}, f32[64,1,128]{2,1,0:T(1,128)S(1)}, u32[]{:S(2)}, u32[]{:S(2)}) collective-permute-start(f32[64,1,128]{2,1,0:T(1,128)S(1)} %get-tuple-element.100), channel_id=1, source_target_pairs={{4,0},{8,4},{12,8},{16,12},{20,16},{24,20},{28,24},{5,1},{9,5},{13... | collective-permute-start | bytes 98312 | tf_op jit(solution)/shard_map/ppermute | solution.py:27
  39.3 17.9 %copy-start.4 = (f32[64,1,128]{2,1,0:T(1,128)}, f32[64,1,128]{2,1,0:T(1,128)S(1)}, u32[]{:S(2)}) copy-start(f32[64,1,128]{2,1,0:T(1,128)S(1)} %collective-permute-done.3) | copy-start | bytes 98308
  39.4 9.2 %copy-start.3 = (f32[39,2048]{1,0:T(8,128)S(1)}, f32[39,2048]{1,0:T(8,128)}, u32[]{:S(2)}) copy-start(f32[39,2048]{1,0:T(8,128)} %param.13) | copy-start | bytes 958468
  40.5 12.6 %collective-permute-start.4 = (f32[64,10,1]{2,1,0:T(8,128)}, f32[64,10,1]{2,1,0:T(8,128)S(1)}, u32[]{:S(2)}, u32[]{:S(2)}) collective-permute-start(f32[64,10,1]{2,1,0:T(8,128)} %get-tuple-element.90), channel_id=1, source_target_pairs={{0,1},{1,2},{2,3},{4,5},{5,6},{6,7},{8,9},{9,10},{10,11},{12,13},{... | collective-permute-start | bytes 7688 | tf_op jit(solution)/shard_map/ppermute | solution.py:25
  46.7 10.5 %collective-permute-start.5 = (f32[64,10,1]{2,1,0:T(8,128)S(1)}, f32[64,10,1]{2,1,0:T(8,128)S(1)}, u32[]{:S(2)}, u32[]{:S(2)}) collective-permute-start(f32[64,10,1]{2,1,0:T(8,128)S(1)} %get-tuple-element.89), channel_id=1, source_target_pairs={{1,0},{2,1},{3,2},{5,4},{6,5},{7,6},{9,8},{10,9},{11,10},{13,12},{... | collective-permute-start | bytes 7688 | tf_op jit(solution)/shard_map/ppermute | solution.py:27
  59.3 6.4 %collective-permute-start.6 = (f32[64,1,128]{2,1,0:T(1,128)S(1)}, f32[64,1,128]{2,1,0:T(1,128)S(1)}, u32[]{:S(2)}, u32[]{:S(2)}) collective-permute-start(f32[64,1,128]{2,1,0:T(1,128)S(1)} %get-tuple-element.97), channel_id=1, source_target_pairs={{0,4},{4,8},{8,12},{12,16},{16,20},{20,24},{24,28},{1,5},{5,9},{9,... | collective-permute-start | bytes 98312 | tf_op jit(solution)/shard_map/ppermute | solution.py:25
  63.3 4.7 %collective-permute-start.7 = (f32[64,1,128]{2,1,0:T(1,128)S(1)}, f32[64,1,128]{2,1,0:T(1,128)S(1)}, u32[]{:S(2)}, u32[]{:S(2)}) collective-permute-start(f32[64,1,128]{2,1,0:T(1,128)S(1)} %get-tuple-element.98), channel_id=1, source_target_pairs={{4,0},{8,4},{12,8},{16,12},{20,16},{24,20},{28,24},{5,1},{9,5},{13... | collective-permute-start | bytes 98312 | tf_op jit(solution)/shard_map/ppermute | solution.py:27
  68.1 11.2 %all-to-all-start = ((f32[8,1,1248]{2,1,0:T(1,128)}), f32[8,1,1248]{2,1,0:T(1,128)S(1)}, u32[]{:S(2)}, u32[]{:S(2)}) async-start(f32[8,1,1248]{2,1,0:T(1,128)} %reshape.58), calls=%async_computation | async-start | bytes 81920 | tf_op jit(solution)/shard_map/all_to_all | solution.py:121
  72.6 9.6 %collective-permute-start.8 = (f32[64,10,1]{2,1,0:T(8,128)S(1)}, f32[64,10,1]{2,1,0:T(8,128)S(1)}, u32[]{:S(2)}, u32[]{:S(2)}) collective-permute-start(f32[64,10,1]{2,1,0:T(8,128)S(1)} %get-tuple-element.88), channel_id=1, source_target_pairs={{0,1},{1,2},{2,3},{4,5},{5,6},{6,7},{8,9},{9,10},{10,11},{12,13},{... | collective-permute-start | bytes 7688 | tf_op jit(solution)/shard_map/ppermute | solution.py:25
  76.1 10.5 %collective-permute-start.9 = (f32[64,10,1]{2,1,0:T(8,128)S(1)}, f32[64,10,1]{2,1,0:T(8,128)S(1)}, u32[]{:S(2)}, u32[]{:S(2)}) collective-permute-start(f32[64,10,1]{2,1,0:T(8,128)S(1)} %get-tuple-element.87), channel_id=1, source_target_pairs={{1,0},{2,1},{3,2},{5,4},{6,5},{7,6},{9,8},{10,9},{11,10},{13,12},{... | collective-permute-start | bytes 7688 | tf_op jit(solution)/shard_map/ppermute | solution.py:27
  88.0 5.3 %collective-permute-start.10 = (f32[64,1,128]{2,1,0:T(1,128)S(1)}, f32[64,1,128]{2,1,0:T(1,128)S(1)}, u32[]{:S(2)}, u32[]{:S(2)}) collective-permute-start(f32[64,1,128]{2,1,0:T(1,128)S(1)} %get-tuple-element.95), channel_id=1, source_target_pairs={{0,4},{4,8},{8,12},{12,16},{16,20},{20,24},{24,28},{1,5},{5,9},{9,... | collective-permute-start | bytes 98312 | tf_op jit(solution)/shard_map/ppermute | solution.py:25
  91.7 4.7 %collective-permute-start.11 = (f32[64,1,128]{2,1,0:T(1,128)S(1)}, f32[64,1,128]{2,1,0:T(1,128)S(1)}, u32[]{:S(2)}, u32[]{:S(2)}) collective-permute-start(f32[64,1,128]{2,1,0:T(1,128)S(1)} %get-tuple-element.96), channel_id=1, source_target_pairs={{4,0},{8,4},{12,8},{16,12},{20,16},{24,20},{28,24},{5,1},{9,5},{13... | collective-permute-start | bytes 98312 | tf_op jit(solution)/shard_map/ppermute | solution.py:27
  96.7 9.2 %collective-permute-start.12 = (f32[64,10,1]{2,1,0:T(8,128)S(1)}, f32[64,10,1]{2,1,0:T(8,128)S(1)}, u32[]{:S(2)}, u32[]{:S(2)}) collective-permute-start(f32[64,10,1]{2,1,0:T(8,128)S(1)} %get-tuple-element.86), channel_id=1, source_target_pairs={{0,1},{1,2},{2,3},{4,5},{5,6},{6,7},{8,9},{9,10},{10,11},{12,13},{... | collective-permute-start | bytes 7688 | tf_op jit(solution)/shard_map/ppermute | solution.py:25
  99.8 10.5 %collective-permute-start.13 = (f32[64,10,1]{2,1,0:T(8,128)S(1)}, f32[64,10,1]{2,1,0:T(8,128)S(1)}, u32[]{:S(2)}, u32[]{:S(2)}) collective-permute-start(f32[64,10,1]{2,1,0:T(8,128)S(1)} %get-tuple-element.85), channel_id=1, source_target_pairs={{1,0},{2,1},{3,2},{5,4},{6,5},{7,6},{9,8},{10,9},{11,10},{13,12},{... | collective-permute-start | bytes 7688 | tf_op jit(solution)/shard_map/ppermute | solution.py:27
  111.6 5.6 %collective-permute-start.14 = (f32[64,1,128]{2,1,0:T(1,128)S(1)}, f32[64,1,128]{2,1,0:T(1,128)S(1)}, u32[]{:S(2)}, u32[]{:S(2)}) collective-permute-start(f32[64,1,128]{2,1,0:T(1,128)S(1)} %get-tuple-element.93), channel_id=1, source_target_pairs={{0,4},{4,8},{8,12},{12,16},{16,20},{20,24},{24,28},{1,5},{5,9},{9,... | collective-permute-start | bytes 98312 | tf_op jit(solution)/shard_map/ppermute | solution.py:25
  115.7 4.7 %collective-permute-start.15 = (f32[64,1,128]{2,1,0:T(1,128)S(1)}, f32[64,1,128]{2,1,0:T(1,128)S(1)}, u32[]{:S(2)}, u32[]{:S(2)}) collective-permute-start(f32[64,1,128]{2,1,0:T(1,128)S(1)} %get-tuple-element.94), channel_id=1, source_target_pairs={{4,0},{8,4},{12,8},{16,12},{20,16},{24,20},{28,24},{5,1},{9,5},{13... | collective-permute-start | bytes 98312 | tf_op jit(solution)/shard_map/ppermute | solution.py:27
  120.6 9.2 %collective-permute-start.16 = (f32[64,10,1]{2,1,0:T(8,128)S(1)}, f32[64,10,1]{2,1,0:T(8,128)S(1)}, u32[]{:S(2)}, u32[]{:S(2)}) collective-permute-start(f32[64,10,1]{2,1,0:T(8,128)S(1)} %get-tuple-element.84), channel_id=1, source_target_pairs={{0,1},{1,2},{2,3},{4,5},{5,6},{6,7},{8,9},{9,10},{10,11},{12,13},{... | collective-permute-start | bytes 7688 | tf_op jit(solution)/shard_map/ppermute | solution.py:25
  123.7 10.5 %collective-permute-start.17 = (f32[64,10,1]{2,1,0:T(8,128)S(1)}, f32[64,10,1]{2,1,0:T(8,128)S(1)}, u32[]{:S(2)}, u32[]{:S(2)}) collective-permute-start(f32[64,10,1]{2,1,0:T(8,128)S(1)} %get-tuple-element.83), channel_id=1, source_target_pairs={{1,0},{2,1},{3,2},{5,4},{6,5},{7,6},{9,8},{10,9},{11,10},{13,12},{... | collective-permute-start | bytes 7688 | tf_op jit(solution)/shard_map/ppermute | solution.py:27
  (8 other events, 17.3 us)
where the time goes:
time: 137 us; the launch traced here: 136 us
  starting transfers between devices  59.8 us (44%)
  waiting for transfers between devices  41.1 us (30%)
  matrix products  11.8 us (9%)
  other arithmetic  9.87 us (7%)
  local copies, waits for them, and re-layouts  8.97 us (7%)
  loops' own time  2.72 us (2%)
  between operations  1.92 us (1%)
    ppermute x8, starting transfers between devices, with_halo(): lax.ppermute(tail, axis, [(i, (i + 1) % count) for i in range(ends)])  31 us
    ppermute x8, waiting for transfers between devices, with_halo(): lax.ppermute(head, axis, [((i + 1) % count, i) for i in range(ends)])  29 us
    ppermute x8, starting transfers between devices, with_halo(): lax.ppermute(head, axis, [((i + 1) % count, i) for i in range(ends)])  12.9 us
    ppermute x8, waiting for transfers between devices, with_halo(): lax.ppermute(tail, axis, [(i, (i + 1) % count) for i in range(ends)])  12.1 us
    all_to_all x1, starting transfers between devices, shards(): lax.all_to_all(occupied, 'gx', split_axis=1, concat_axis=1, tiled=True)  6.4 us
    dot_general x4, matrix products, one_block(): lax.dot_general(left_table, right_table, (((0,), (0,)), ((), ())), prefer...  6.01 us
    ppermute x2, starting transfers between devices, shifted(): return lax.ppermute(block, axis, route)  5.28 us
    dot_general x8, matrix products, network_rates(): jnp.dot(coupling, occupancy, precision=lax.Precision.HIGHEST, preferred_e...  5.17 us
  transfers between devices with their start and end apart: 20, of which 12 were waited for; matrix products, arithmetic and copies ran while one was open for 8% of the time, Pallas kernels for 0%

commit v1 on v0

--- a/solution.py
+++ b/solution.py
@@ -3,9 +3,15 @@
 import jax.numpy as jnp
 from jax import lax
 from jax.sharding import PartitionSpec as P
+from jax.lax import all_to_all, psum
 
 time_step = 0.25
 diffusion_number = 0.16
+
+
+def slabs_serve(mine, mesh_ax):
+    state_now = all_to_all(jnp.stack(jnp.split(mine, psum(1, mesh_ax), axis=1)), mesh_ax, 0, 0)
+    return jnp.concatenate(state_now, axis=1)
 
 
 def shifted(block, axis, distance):
@@ -118,7 +124,7 @@
     )
     occupied = jnp.sum(placing, axis=0)[None, :]
     received, arrived = (
-        lax.all_to_all(outgoing, "gx", split_axis=1, concat_axis=1, tiled=True),
+        slabs_serve(outgoing, "gx"),
         lax.all_to_all(occupied, "gx", split_axis=1, concat_axis=1, tiled=True),
     )
     new_state = advance(cell_state, coupling, basal_rate, half_sat, decay_rate)

time: 137 us -> 137 us (level)
  transfers between devices with their start and end apart: 20 -> 20, of which waited for: 12 -> 12; matrix products, arithmetic and copies ran while one was open for 8% -> 7% of each run, Pallas kernels for 0% -> 0%
where the time goes in v1:
time: 137 us; the launch traced here: 136 us
  starting transfers between devices  59.9 us (44%)
  waiting for transfers between devices  42.2 us (31%)
  matrix products  11.8 us (9%)
  other arithmetic  9.07 us (7%)
  local copies, waits for them, and re-layouts  8.7 us (6%)
  loops' own time  2.72 us (2%)
  between operations  1.91 us (1%)
    ppermute x8, starting transfers between devices, with_halo(): lax.ppermute(tail, axis, [(i, (i + 1) % count) for i in range(ends)])  31.2 us
    ppermute x8, waiting for transfers between devices, with_halo(): lax.ppermute(head, axis, [((i + 1) % count, i) for i in range(ends)])  29.4 us
    ppermute x8, starting transfers between devices, with_halo(): lax.ppermute(head, axis, [((i + 1) % count, i) for i in range(ends)])  12.9 us
    ppermute x8, waiting for transfers between devices, with_halo(): lax.ppermute(tail, axis, [(i, (i + 1) % count) for i in range(ends)])  12.7 us
    all_to_all x1, starting transfers between devices, shards(): lax.all_to_all(occupied, 'gx', split_axis=1, concat_axis=1, tiled=True)  6.39 us
    dot_general x4, matrix products, one_block(): lax.dot_general(left_table, right_table, (((0,), (0,)), ((), ())), prefer...  6.01 us
    ppermute x2, starting transfers between devices, shifted(): return lax.ppermute(block, axis, route)  5.28 us
    dot_general x8, matrix products, network_rates(): jnp.dot(coupling, occupancy, precision=lax.Precision.HIGHEST, preferred_e...  5.17 us
  transfers between devices with their start and end apart: 20, of which 12 were waited for; matrix products, arithmetic and copies ran while one was open for 7% of the time, Pallas kernels for 0%

profile of v1, /device:TPU:1, one launch (start us, length us, event | category | flops | bytes accessed | tf_op | source)
XLA Modules:
  0.0 136.2 jit_solution(12604600258027304712)
XLA Ops:
  6.1 12.0 %while.11 = (s32[]{:T(128)}, f32[1536,128]{1,0:T(8,128)S(1)}, s32[4]{0:T(128)S(1)}, s32[2048]{0:T(1024)S(1)}, s32[2048]{0:T(1024)S(1)}, /*index=5*/bf16[2048]{0:...) while((s32[]{:T(128)}, f32[1536,128]{1,0:T(8,128)S(1)}, s32[4]{0:T(128)S(1)}, ...), condition=%wide.region_4.5_spmd.clone, body=%wide.region_3.4_spmd.clone.sunk | while | flops 202637312 | bytes 1588405 | solution.py:80
  18.2 4.0 %collective-permute-start = (bf16[64,8,128]{2,1,0:T(8,128)(2,1)S(1)}, bf16[64,8,128]{2,1,0:T(8,128)(2,1)S(1)}, u32[]{:S(2)}, u32[]{:S(2)}) collective-permute-start(bf16[64,8,128]{2,1,0:T(8,128)(2,1)S(1)} %get-tuple-element.91), channel_id=1, source_target_pairs={{0,4},{4,8},{8,12},{12,16},{16,20},{20,24},{24,28},{1,5},{5,9},{9,... | collective-permute-start | bytes 393224 | tf_op jit(solution)/shard_map/ppermute | solution.py:20
  24.7 6.4 %all-to-all-start.1 = ((f32[1,8,32]{2,0,1:T(1,128)}), f32[1,8,32]{2,0,1:T(1,128)S(1)}, u32[]{:S(2)}, u32[]{:S(2)}) async-start(f32[1,8,32]{2,0,1:T(1,128)} %all_to_all.10), calls=%async_computation.1 | async-start | bytes 8192 | tf_op jit(solution)/shard_map/all_to_all | solution.py:128
  32.9 3.4 %collective-permute-start.2 = (f32[64,1,128]{2,1,0:T(1,128)S(1)}, f32[64,1,128]{2,1,0:T(1,128)S(1)}, u32[]{:S(2)}, u32[]{:S(2)}) collective-permute-start(f32[64,1,128]{2,1,0:T(1,128)S(1)} %get-tuple-element.99), channel_id=1, source_target_pairs={{0,4},{4,8},{8,12},{12,16},{16,20},{20,24},{24,28},{1,5},{5,9},{9,... | collective-permute-start | bytes 98312 | tf_op jit(solution)/shard_map/ppermute | solution.py:31
  37.6 3.3 %collective-permute-done.3 = f32[64,1,128]{2,1,0:T(1,128)S(1)} collective-permute-done((f32[64,1,128]{2,1,0:T(1,128)S(1)}, f32[64,1,128]{2,1,0:T(1,128)S(1)}, u32[]{:S(2)}, u32[]{:S(2)}) %collective-permute-start.3) | collective-permute-done | bytes 32800 | tf_op jit(solution)/shard_map/ppermute | solution.py:33
  41.2 6.2 %collective-permute-start.4 = (f32[64,10,1]{2,1,0:T(8,128)S(1)}, f32[64,10,1]{2,1,0:T(8,128)S(1)}, u32[]{:S(2)}, u32[]{:S(2)}) collective-permute-start(f32[64,10,1]{2,1,0:T(8,128)S(1)} %get-tuple-element.90), channel_id=1, source_target_pairs={{0,1},{1,2},{2,3},{4,5},{5,6},{6,7},{8,9},{9,10},{10,11},{12,13},{... | collective-permute-start | bytes 7688 | tf_op jit(solution)/shard_map/ppermute | solution.py:31
  49.4 4.1 %collective-permute-done.4 = f32[64,10,1]{2,1,0:T(8,128)S(1)} collective-permute-done((f32[64,10,1]{2,1,0:T(8,128)S(1)}, f32[64,10,1]{2,1,0:T(8,128)S(1)}, u32[]{:S(2)}, u32[]{:S(2)}) %collective-permute-start.4) | collective-permute-done | bytes 2592 | tf_op jit(solution)/shard_map/ppermute | solution.py:31
  53.6 4.4 %collective-permute-done.5 = f32[64,10,1]{2,1,0:T(8,128)S(1)} collective-permute-done((f32[64,10,1]{2,1,0:T(8,128)S(1)}, f32[64,10,1]{2,1,0:T(8,128)S(1)}, u32[]{:S(2)}, u32[]{:S(2)}) %collective-permute-start.5) | collective-permute-done | bytes 2592 | tf_op jit(solution)/shard_map/ppermute | solution.py:33
  59.3 4.1 %collective-permute-start.6 = (f32[64,1,128]{2,1,0:T(1,128)S(1)}, f32[64,1,128]{2,1,0:T(1,128)S(1)}, u32[]{:S(2)}, u32[]{:S(2)}) collective-permute-start(f32[64,1,128]{2,1,0:T(1,128)S(1)} %get-tuple-element.97), channel_id=1, source_target_pairs={{0,4},{4,8},{8,12},{12,16},{16,20},{20,24},{24,28},{1,5},{5,9},{9,... | collective-permute-start | bytes 98312 | tf_op jit(solution)/shard_map/ppermute | solution.py:31
  65.7 2.4 %collective-permute-done.7 = f32[64,1,128]{2,1,0:T(1,128)S(1)} collective-permute-done((f32[64,1,128]{2,1,0:T(1,128)S(1)}, f32[64,1,128]{2,1,0:T(1,128)S(1)}, u32[]{:S(2)}, u32[]{:S(2)}) %collective-permute-start.7) | collective-permute-done | bytes 32800 | tf_op jit(solution)/shard_map/ppermute | solution.py:33
  68.1 4.2 %all-to-all-start = ((f32[8,1,1248]{2,1,0:T(1,128)}), f32[8,1,1248]{2,1,0:T(1,128)S(1)}, u32[]{:S(2)}, u32[]{:S(2)}) async-start(f32[8,1,1248]{2,1,0:T(1,128)} %reshape.64), calls=%async_computation | async-start | bytes 81920 | tf_op jit(solution)/shard_map/all_to_all | solution.py:13
  72.5 3.5 %collective-permute-start.8 = (f32[64,10,1]{2,1,0:T(8,128)S(1)}, f32[64,10,1]{2,1,0:T(8,128)S(1)}, u32[]{:S(2)}, u32[]{:S(2)}) collective-permute-start(f32[64,10,1]{2,1,0:T(8,128)S(1)} %get-tuple-element.88), channel_id=1, source_target_pairs={{0,1},{1,2},{2,3},{4,5},{5,6},{6,7},{8,9},{9,10},{10,11},{12,13},{... | collective-permute-start | bytes 7688 | tf_op jit(solution)/shard_map/ppermute | solution.py:31
  82.1 4.4 %collective-permute-done.9 = f32[64,10,1]{2,1,0:T(8,128)S(1)} collective-permute-done((f32[64,10,1]{2,1,0:T(8,128)S(1)}, f32[64,10,1]{2,1,0:T(8,128)S(1)}, u32[]{:S(2)}, u32[]{:S(2)}) %collective-permute-start.9) | collective-permute-done | bytes 2592 | tf_op jit(solution)/shard_map/ppermute | solution.py:33
  87.9 3.7 %collective-permute-start.10 = (f32[64,1,128]{2,1,0:T(1,128)S(1)}, f32[64,1,128]{2,1,0:T(1,128)S(1)}, u32[]{:S(2)}, u32[]{:S(2)}) collective-permute-start(f32[64,1,128]{2,1,0:T(1,128)S(1)} %get-tuple-element.95), channel_id=1, source_target_pairs={{0,4},{4,8},{8,12},{12,16},{16,20},{20,24},{24,28},{1,5},{5,9},{9,... | collective-permute-start | bytes 98312 | tf_op jit(solution)/shard_map/ppermute | solution.py:31
  93.2 3.1 %collective-permute-done.11 = f32[64,1,128]{2,1,0:T(1,128)S(1)} collective-permute-done((f32[64,1,128]{2,1,0:T(1,128)S(1)}, f32[64,1,128]{2,1,0:T(1,128)S(1)}, u32[]{:S(2)}, u32[]{:S(2)}) %collective-permute-start.11) | collective-permute-done | bytes 32800 | tf_op jit(solution)/shard_map/ppermute | solution.py:33
  96.6 3.1 %collective-permute-start.12 = (f32[64,10,1]{2,1,0:T(8,128)S(1)}, f32[64,10,1]{2,1,0:T(8,128)S(1)}, u32[]{:S(2)}, u32[]{:S(2)}) collective-permute-start(f32[64,10,1]{2,1,0:T(8,128)S(1)} %get-tuple-element.86), channel_id=1, source_target_pairs={{0,1},{1,2},{2,3},{4,5},{5,6},{6,7},{8,9},{9,10},{10,11},{12,13},{... | collective-permute-start | bytes 7688 | tf_op jit(solution)/shard_map/ppermute | solution.py:31
  99.7 1.9 %collective-permute-start.13 = (f32[64,10,1]{2,1,0:T(8,128)S(1)}, f32[64,10,1]{2,1,0:T(8,128)S(1)}, u32[]{:S(2)}, u32[]{:S(2)}) collective-permute-start(f32[64,10,1]{2,1,0:T(8,128)S(1)} %get-tuple-element.85), channel_id=1, source_target_pairs={{1,0},{2,1},{3,2},{5,4},{6,5},{7,6},{9,8},{10,9},{11,10},{13,12},{... | collective-permute-start | bytes 7688 | tf_op jit(solution)/shard_map/ppermute | solution.py:33
  101.9 3.9 %collective-permute-done.12 = f32[64,10,1]{2,1,0:T(8,128)S(1)} collective-permute-done((f32[64,10,1]{2,1,0:T(8,128)S(1)}, f32[64,10,1]{2,1,0:T(8,128)S(1)}, u32[]{:S(2)}, u32[]{:S(2)}) %collective-permute-start.12) | collective-permute-done | bytes 2592 | tf_op jit(solution)/shard_map/ppermute | solution.py:31
  105.8 4.4 %collective-permute-done.13 = f32[64,10,1]{2,1,0:T(8,128)S(1)} collective-permute-done((f32[64,10,1]{2,1,0:T(8,128)S(1)}, f32[64,10,1]{2,1,0:T(8,128)S(1)}, u32[]{:S(2)}, u32[]{:S(2)}) %collective-permute-start.13) | collective-permute-done | bytes 2592 | tf_op jit(solution)/shard_map/ppermute | solution.py:33
  111.6 4.1 %collective-permute-start.14 = (f32[64,1,128]{2,1,0:T(1,128)S(1)}, f32[64,1,128]{2,1,0:T(1,128)S(1)}, u32[]{:S(2)}, u32[]{:S(2)}) collective-permute-start(f32[64,1,128]{2,1,0:T(1,128)S(1)} %get-tuple-element.93), channel_id=1, source_target_pairs={{0,4},{4,8},{8,12},{12,16},{16,20},{20,24},{24,28},{1,5},{5,9},{9,... | collective-permute-start | bytes 98312 | tf_op jit(solution)/shard_map/ppermute | solution.py:31
  117.2 3.1 %collective-permute-done.15 = f32[64,1,128]{2,1,0:T(1,128)S(1)} collective-permute-done((f32[64,1,128]{2,1,0:T(1,128)S(1)}, f32[64,1,128]{2,1,0:T(1,128)S(1)}, u32[]{:S(2)}, u32[]{:S(2)}) %collective-permute-start.15) | collective-permute-done | bytes 32800 | tf_op jit(solution)/shard_map/ppermute | solution.py:33
  120.6 3.1 %collective-permute-start.16 = (f32[64,10,1]{2,1,0:T(8,128)S(1)}, f32[64,10,1]{2,1,0:T(8,128)S(1)}, u32[]{:S(2)}, u32[]{:S(2)}) collective-permute-start(f32[64,10,1]{2,1,0:T(8,128)S(1)} %get-tuple-element.84), channel_id=1, source_target_pairs={{0,1},{1,2},{2,3},{4,5},{5,6},{6,7},{8,9},{9,10},{10,11},{12,13},{... | collective-permute-start | bytes 7688 | tf_op jit(solution)/shard_map/ppermute | solution.py:31
  126.5 3.3 %collective-permute-done.16 = f32[64,10,1]{2,1,0:T(8,128)S(1)} collective-permute-done((f32[64,10,1]{2,1,0:T(8,128)S(1)}, f32[64,10,1]{2,1,0:T(8,128)S(1)}, u32[]{:S(2)}, u32[]{:S(2)}) %collective-permute-start.16) | collective-permute-done | bytes 2592 | tf_op jit(solution)/shard_map/ppermute | solution.py:31
  129.8 4.4 %collective-permute-done.17 = f32[64,10,1]{2,1,0:T(8,128)S(1)} collective-permute-done((f32[64,10,1]{2,1,0:T(8,128)S(1)}, f32[64,10,1]{2,1,0:T(8,128)S(1)}, u32[]{:S(2)}, u32[]{:S(2)}) %collective-permute-start.17) | collective-permute-done | bytes 2592 | tf_op jit(solution)/shard_map/ppermute | solution.py:33
  (123 shorter events, 43.2 us)
Async XLA Ops:
  0.6 2.5 %copy-start.2 = (f32[39,2048]{1,0:T(8,128)S(1)}, f32[39,2048]{1,0:T(8,128)}, u32[]{:S(2)}) copy-start(f32[39,2048]{1,0:T(8,128)} %param.13) | copy-start | bytes 958468
  18.1 5.4 %copy-start.5 = (s32[128,1]{0,1:T(1,128)S(1)}, s32[128,1]{0,1:T(1,128)}, u32[]{:S(2)}) copy-start(s32[128,1]{0,1:T(1,128)} %param.21) | copy-start | bytes 1540
  18.1 13.4 %copy-start.7 = (s32[128]{0:T(128)S(1)}, s32[128]{0:T(128)}, u32[]{:S(2)}) copy-start(s32[128]{0:T(128)} %param.20) | copy-start | bytes 1540
  18.2 14.6 %collective-permute-start = (bf16[64,8,128]{2,1,0:T(8,128)(2,1)S(1)}, bf16[64,8,128]{2,1,0:T(8,128)(2,1)S(1)}, u32[]{:S(2)}, u32[]{:S(2)}) collective-permute-start(bf16[64,8,128]{2,1,0:T(8,128)(2,1)S(1)} %get-tuple-element.91), channel_id=1, source_target_pairs={{0,4},{4,8},{8,12},{12,16},{16,20},{20,24},{24,28},{1,5},{5,9},{9,... | collective-permute-start | bytes 393224 | tf_op jit(solution)/shard_map/ppermute | solution.py:20
  22.2 10.6 %collective-permute-start.1 = (bf16[64,8,128]{2,1,0:T(8,128)(2,1)S(1)}, bf16[64,8,128]{2,1,0:T(8,128)(2,1)S(1)}, u32[]{:S(2)}, u32[]{:S(2)}) collective-permute-start(bf16[64,8,128]{2,1,0:T(8,128)(2,1)S(1)} %get-tuple-element.92), channel_id=1, source_target_pairs={{4,0},{8,4},{12,8},{16,12},{20,16},{24,20},{28,24},{5,1},{9,5},{13... | collective-permute-start | bytes 393224 | tf_op jit(solution)/shard_map/ppermute | solution.py:20
  23.5 9.3 %copy-start.3 = (f32[64,8,128]{2,1,0:T(8,128)S(1)}, f32[64,8,128]{2,1,0:T(8,128)}, u32[]{:S(2)}) copy-start(f32[64,8,128]{2,1,0:T(8,128)} %param.23) | copy-start | bytes 786436
  24.7 43.4 %all-to-all-start.1 = ((f32[1,8,32]{2,0,1:T(1,128)}), f32[1,8,32]{2,0,1:T(1,128)S(1)}, u32[]{:S(2)}, u32[]{:S(2)}) async-start(f32[1,8,32]{2,0,1:T(1,128)} %all_to_all.10), calls=%async_computation.1 | async-start | bytes 8192 | tf_op jit(solution)/shard_map/all_to_all | solution.py:128
  32.9 4.8 %collective-permute-start.2 = (f32[64,1,128]{2,1,0:T(1,128)S(1)}, f32[64,1,128]{2,1,0:T(1,128)S(1)}, u32[]{:S(2)}, u32[]{:S(2)}) collective-permute-start(f32[64,1,128]{2,1,0:T(1,128)S(1)} %get-tuple-element.99), channel_id=1, source_target_pairs={{0,4},{4,8},{8,12},{12,16},{16,20},{20,24},{24,28},{1,5},{5,9},{9,... | collective-permute-start | bytes 98312 | tf_op jit(solution)/shard_map/ppermute | solution.py:31
  36.2 4.7 %collective-permute-start.3 = (f32[64,1,128]{2,1,0:T(1,128)S(1)}, f32[64,1,128]{2,1,0:T(1,128)S(1)}, u32[]{:S(2)}, u32[]{:S(2)}) collective-permute-start(f32[64,1,128]{2,1,0:T(1,128)S(1)} %get-tuple-element.100), channel_id=1, source_target_pairs={{4,0},{8,4},{12,8},{16,12},{20,16},{24,20},{28,24},{5,1},{9,5},{13... | collective-permute-start | bytes 98312 | tf_op jit(solution)/shard_map/ppermute | solution.py:33
  41.2 12.3 %collective-permute-start.4 = (f32[64,10,1]{2,1,0:T(8,128)S(1)}, f32[64,10,1]{2,1,0:T(8,128)S(1)}, u32[]{:S(2)}, u32[]{:S(2)}) collective-permute-start(f32[64,10,1]{2,1,0:T(8,128)S(1)} %get-tuple-element.90), channel_id=1, source_target_pairs={{0,1},{1,2},{2,3},{4,5},{5,6},{6,7},{8,9},{9,10},{10,11},{12,13},{... | collective-permute-start | bytes 7688 | tf_op jit(solution)/shard_map/ppermute | solution.py:31
  47.4 10.5 %collective-permute-start.5 = (f32[64,10,1]{2,1,0:T(8,128)S(1)}, f32[64,10,1]{2,1,0:T(8,128)S(1)}, u32[]{:S(2)}, u32[]{:S(2)}) collective-permute-start(f32[64,10,1]{2,1,0:T(8,128)S(1)} %get-tuple-element.89), channel_id=1, source_target_pairs={{1,0},{2,1},{3,2},{5,4},{6,5},{7,6},{9,8},{10,9},{11,10},{13,12},{... | collective-permute-start | bytes 7688 | tf_op jit(solution)/shard_map/ppermute | solution.py:33
  59.3 6.4 %collective-permute-start.6 = (f32[64,1,128]{2,1,0:T(1,128)S(1)}, f32[64,1,128]{2,1,0:T(1,128)S(1)}, u32[]{:S(2)}, u32[]{:S(2)}) collective-permute-start(f32[64,1,128]{2,1,0:T(1,128)S(1)} %get-tuple-element.97), channel_id=1, source_target_pairs={{0,4},{4,8},{8,12},{12,16},{16,20},{20,24},{24,28},{1,5},{5,9},{9,... | collective-permute-start | bytes 98312 | tf_op jit(solution)/shard_map/ppermute | solution.py:31
  63.4 4.7 %collective-permute-start.7 = (f32[64,1,128]{2,1,0:T(1,128)S(1)}, f32[64,1,128]{2,1,0:T(1,128)S(1)}, u32[]{:S(2)}, u32[]{:S(2)}) collective-permute-start(f32[64,1,128]{2,1,0:T(1,128)S(1)} %get-tuple-element.98), channel_id=1, source_target_pairs={{4,0},{8,4},{12,8},{16,12},{20,16},{24,20},{28,24},{5,1},{9,5},{13... | collective-permute-start | bytes 98312 | tf_op jit(solution)/shard_map/ppermute | solution.py:33
  68.1 11.1 %all-to-all-start = ((f32[8,1,1248]{2,1,0:T(1,128)}), f32[8,1,1248]{2,1,0:T(1,128)S(1)}, u32[]{:S(2)}, u32[]{:S(2)}) async-start(f32[8,1,1248]{2,1,0:T(1,128)} %reshape.64), calls=%async_computation | async-start | bytes 81920 | tf_op jit(solution)/shard_map/all_to_all | solution.py:13
  72.5 9.6 %collective-permute-start.8 = (f32[64,10,1]{2,1,0:T(8,128)S(1)}, f32[64,10,1]{2,1,0:T(8,128)S(1)}, u32[]{:S(2)}, u32[]{:S(2)}) collective-permute-start(f32[64,10,1]{2,1,0:T(8,128)S(1)} %get-tuple-element.88), channel_id=1, source_target_pairs={{0,1},{1,2},{2,3},{4,5},{5,6},{6,7},{8,9},{9,10},{10,11},{12,13},{... | collective-permute-start | bytes 7688 | tf_op jit(solution)/shard_map/ppermute | solution.py:31
  76.0 10.5 %collective-permute-start.9 = (f32[64,10,1]{2,1,0:T(8,128)S(1)}, f32[64,10,1]{2,1,0:T(8,128)S(1)}, u32[]{:S(2)}, u32[]{:S(2)}) collective-permute-start(f32[64,10,1]{2,1,0:T(8,128)S(1)} %get-tuple-element.87), channel_id=1, source_target_pairs={{1,0},{2,1},{3,2},{5,4},{6,5},{7,6},{9,8},{10,9},{11,10},{13,12},{... | collective-permute-start | bytes 7688 | tf_op jit(solution)/shard_map/ppermute | solution.py:33
  87.9 5.3 %collective-permute-start.10 = (f32[64,1,128]{2,1,0:T(1,128)S(1)}, f32[64,1,128]{2,1,0:T(1,128)S(1)}, u32[]{:S(2)}, u32[]{:S(2)}) collective-permute-start(f32[64,1,128]{2,1,0:T(1,128)S(1)} %get-tuple-element.95), channel_id=1, source_target_pairs={{0,4},{4,8},{8,12},{12,16},{16,20},{20,24},{24,28},{1,5},{5,9},{9,... | collective-permute-start | bytes 98312 | tf_op jit(solution)/shard_map/ppermute | solution.py:31
  91.7 4.7 %collective-permute-start.11 = (f32[64,1,128]{2,1,0:T(1,128)S(1)}, f32[64,1,128]{2,1,0:T(1,128)S(1)}, u32[]{:S(2)}, u32[]{:S(2)}) collective-permute-start(f32[64,1,128]{2,1,0:T(1,128)S(1)} %get-tuple-element.96), channel_id=1, source_target_pairs={{4,0},{8,4},{12,8},{16,12},{20,16},{24,20},{28,24},{5,1},{9,5},{13... | collective-permute-start | bytes 98312 | tf_op jit(solution)/shard_map/ppermute | solution.py:33
  96.6 9.2 %collective-permute-start.12 = (f32[64,10,1]{2,1,0:T(8,128)S(1)}, f32[64,10,1]{2,1,0:T(8,128)S(1)}, u32[]{:S(2)}, u32[]{:S(2)}) collective-permute-start(f32[64,10,1]{2,1,0:T(8,128)S(1)} %get-tuple-element.86), channel_id=1, source_target_pairs={{0,1},{1,2},{2,3},{4,5},{5,6},{6,7},{8,9},{9,10},{10,11},{12,13},{... | collective-permute-start | bytes 7688 | tf_op jit(solution)/shard_map/ppermute | solution.py:31
  99.7 10.5 %collective-permute-start.13 = (f32[64,10,1]{2,1,0:T(8,128)S(1)}, f32[64,10,1]{2,1,0:T(8,128)S(1)}, u32[]{:S(2)}, u32[]{:S(2)}) collective-permute-start(f32[64,10,1]{2,1,0:T(8,128)S(1)} %get-tuple-element.85), channel_id=1, source_target_pairs={{1,0},{2,1},{3,2},{5,4},{6,5},{7,6},{9,8},{10,9},{11,10},{13,12},{... | collective-permute-start | bytes 7688 | tf_op jit(solution)/shard_map/ppermute | solution.py:33
  111.6 5.6 %collective-permute-start.14 = (f32[64,1,128]{2,1,0:T(1,128)S(1)}, f32[64,1,128]{2,1,0:T(1,128)S(1)}, u32[]{:S(2)}, u32[]{:S(2)}) collective-permute-start(f32[64,1,128]{2,1,0:T(1,128)S(1)} %get-tuple-element.93), channel_id=1, source_target_pairs={{0,4},{4,8},{8,12},{12,16},{16,20},{20,24},{24,28},{1,5},{5,9},{9,... | collective-permute-start | bytes 98312 | tf_op jit(solution)/shard_map/ppermute | solution.py:31
  115.6 4.7 %collective-permute-start.15 = (f32[64,1,128]{2,1,0:T(1,128)S(1)}, f32[64,1,128]{2,1,0:T(1,128)S(1)}, u32[]{:S(2)}, u32[]{:S(2)}) collective-permute-start(f32[64,1,128]{2,1,0:T(1,128)S(1)} %get-tuple-element.94), channel_id=1, source_target_pairs={{4,0},{8,4},{12,8},{16,12},{20,16},{24,20},{28,24},{5,1},{9,5},{13... | collective-permute-start | bytes 98312 | tf_op jit(solution)/shard_map/ppermute | solution.py:33
  120.6 9.2 %collective-permute-start.16 = (f32[64,10,1]{2,1,0:T(8,128)S(1)}, f32[64,10,1]{2,1,0:T(8,128)S(1)}, u32[]{:S(2)}, u32[]{:S(2)}) collective-permute-start(f32[64,10,1]{2,1,0:T(8,128)S(1)} %get-tuple-element.84), channel_id=1, source_target_pairs={{0,1},{1,2},{2,3},{4,5},{5,6},{6,7},{8,9},{9,10},{10,11},{12,13},{... | collective-permute-start | bytes 7688 | tf_op jit(solution)/shard_map/ppermute | solution.py:31
  123.7 10.5 %collective-permute-start.17 = (f32[64,10,1]{2,1,0:T(8,128)S(1)}, f32[64,10,1]{2,1,0:T(8,128)S(1)}, u32[]{:S(2)}, u32[]{:S(2)}) collective-permute-start(f32[64,10,1]{2,1,0:T(8,128)S(1)} %get-tuple-element.83), channel_id=1, source_target_pairs={{1,0},{2,1},{3,2},{5,4},{6,5},{7,6},{9,8},{10,9},{11,10},{13,12},{... | collective-permute-start | bytes 7688 | tf_op jit(solution)/shard_map/ppermute | solution.py:33
  (6 other events, 9.4 us)
